TPU v7x, 32 devices: a whole 2x2x4 slice. The times are simulated.
32 devices in a mesh: dp: 16 (over z, y, x), tensor: 2 (over core).
Axes of the slice: x: 2, y: 2, z: 4, core: 2. Of those that a mesh axis runs over, the one named last changes fastest.
Arguments:
- text_input: bfloat16 [32, 512, 768], P(('dp', 'tensor')), may hold values from -6 to 6
- layout_input: bfloat16 [32, 512, 192], P(('dp', 'tensor')), may hold values from -6 to 6
- page_counts: int32 [32], P(('dp', 'tensor')), may hold values from 16 to 512, as said below
- text_joint: bfloat16 [768, 2304], replicated, may hold values from -0.21875 to 0.21875
- text_mixing: bfloat16 [768, 768], replicated, may hold values from -0.625 to 0.625
- text_norms: float32 [4, 768], replicated, may hold values from 0.1 to 1.9
- text_upward: bfloat16 [768, 3072], P(None, 'tensor'), may hold values from -0.21875 to 0.21875
- text_downward: bfloat16 [3072, 768], P('tensor'), may hold values from -0.109375 to 0.109375
- layout_joint: bfloat16 [192, 576], replicated, may hold values from -0.4375 to 0.4375
- layout_mixing: bfloat16 [192, 192], replicated, may hold values from -1.25 to 1.25
- layout_norms: float32 [4, 192], replicated, may hold values from 0.1 to 1.9
- layout_upward: bfloat16 [192, 768], P(None, 'tensor'), may hold values from -0.4375 to 0.4375
- layout_downward: bfloat16 [768, 192], P('tensor'), may hold values from -0.21875 to 0.21875
- text_cotangent: bfloat16 [32, 512, 768], P(('dp', 'tensor')), may hold values from -6 to 6
- layout_cotangent: bfloat16 [32, 512, 192], P(('dp', 'tensor')), may hold values from -6 to 6
Outputs:
- text_result: bfloat16 [32, 512, 768], P(('dp', 'tensor'))
- layout_result: bfloat16 [32, 512, 192], P(('dp', 'tensor'))
- text_gradient: float32 [32, 512, 768], P(('dp', 'tensor'))
- layout_gradient: float32 [32, 512, 192], P(('dp', 'tensor'))
- joint_text_gradient: float32 [768, 2304], replicated
- mixing_text_gradient: float32 [768, 768], replicated
- norms_text_gradient: float32 [4, 768], replicated
- upward_text_gradient: float32 [768, 3072], P(None, 'tensor')
- downward_text_gradient: float32 [3072, 768], P('tensor')
- joint_layout_gradient: float32 [192, 576], replicated
- mixing_layout_gradient: float32 [192, 192], replicated
- norms_layout_gradient: float32 [4, 192], replicated
- upward_layout_gradient: float32 [192, 768], P(None, 'tensor')
- downward_layout_gradient: float32 [768, 192], P('tensor')
Inputs may be any that keep to these rules, and one draw needn't show every extreme that they name: `page_counts`: keys of a page in slots below its count are live; some page has all 512 slots live; counts are spread over several powers of two.
All inputs are finite; a program needn't handle non-finite values.
Results may differ from a plain program's by a relative error of at most 0.015.
Values may be sent and summed in bfloat16 or wider, within the bound.
No kernel may reach another device: no remote copies, remote signals or barrier semaphores. Data moves between devices by JAX's collectives and lax.ppermute only.
A program may use at most 192 MiB of HBM per device.

v0:
```python
import math
import jax
import jax.numpy as jnp
from jax import lax
from jax.sharding import PartitionSpec as P

HEADS = 12
NEG_FILL = -1e30


def normalize(hidden, gain, shift):
    center = hidden - jnp.mean(hidden, axis=-1, keepdims=True)
    spread = jnp.mean(center * center, axis=-1, keepdims=True)
    return center * lax.rsqrt(spread + 1e-05) * gain + shift


def gelu_exact(value):
    return jax.nn.gelu(value, approximate=False)


def scores_of(queries, keys_in, scale):
    return jnp.einsum("qhd,khd->hqk", queries, keys_in, preferred_element_type=jnp.float32) * scale


def logits_pair(text_grid, layout_grid, count):
    slots = text_grid.shape[0]
    text_score = scores_of(text_grid[:, 0], text_grid[:, 1], 1.0 / math.sqrt(text_grid.shape[-1]))
    layout_score = scores_of(
        layout_grid[:, 0], layout_grid[:, 1], 1.0 / math.sqrt(layout_grid.shape[-1])
    )
    live = (jnp.arange(slots) < count)[None, None, :]
    return (
        jnp.where(live, text_score + layout_score, NEG_FILL),
        jnp.where(live, layout_score + text_score, NEG_FILL),
    )


def attend(logits, values):
    top = jnp.max(logits, axis=-1, keepdims=True)
    total = top + jnp.log(jnp.sum(jnp.exp(logits - top), axis=-1, keepdims=True))
    weights = jnp.exp(logits - total).astype(jnp.bfloat16)
    mixed = jnp.einsum("hqk,khd->qhd", weights, values, preferred_element_type=jnp.float32)
    return (mixed.astype(jnp.bfloat16), total)


def page_forward(items):
    text_grid, layout_grid, count = items
    text_logits, layout_logits = logits_pair(text_grid, layout_grid, count)
    text_mixed, text_total = attend(text_logits, text_grid[:, 2])
    layout_mixed, layout_total = attend(layout_logits, layout_grid[:, 2])
    return (text_mixed, layout_mixed, text_total, layout_total)


def probs_back(logits, total, values, upstream):
    probs = jnp.exp(logits - total)
    value_grad = jnp.einsum(
        "hqk,qhd->khd", probs.astype(jnp.bfloat16), upstream, preferred_element_type=jnp.float32
    )
    prob_grad = jnp.einsum("qhd,khd->hqk", upstream, values, preferred_element_type=jnp.float32)
    logit_grad = probs * (prob_grad - jnp.sum(prob_grad * probs, axis=-1, keepdims=True))
    return (logit_grad, value_grad)


def joint_grads(grid, score_grad, value_grad):
    scale = 1.0 / math.sqrt(grid.shape[-1])
    query_grad = (
        jnp.einsum("hqk,khd->qhd", score_grad, grid[:, 1], preferred_element_type=jnp.float32)
        * scale
    )
    key_grad = (
        jnp.einsum("hqk,qhd->khd", score_grad, grid[:, 0], preferred_element_type=jnp.float32)
        * scale
    )
    return jnp.stack([query_grad, key_grad, value_grad], axis=1).astype(jnp.bfloat16)


def page_backward(items):
    text_grid, layout_grid, count, text_total, layout_total, text_upper, layout_upper = items
    text_logits, layout_logits = logits_pair(text_grid, layout_grid, count)
    text_lgrad, text_vgrad = probs_back(text_logits, text_total, text_grid[:, 2], text_upper)
    layout_lgrad, layout_vgrad = probs_back(
        layout_logits, layout_total, layout_grid[:, 2], layout_upper
    )
    text_sgrad = text_lgrad.astype(jnp.bfloat16)
    layout_sgrad = (text_lgrad + layout_lgrad).astype(jnp.bfloat16)
    return (
        joint_grads(text_grid, text_sgrad, text_vgrad),
        joint_grads(layout_grid, layout_sgrad, layout_vgrad),
    )


def matmul(left, right):
    return jnp.dot(left, right, preferred_element_type=jnp.float32)


def shards(
    text_input,
    layout_input,
    page_counts,
    text_joint,
    text_mixing,
    text_norms,
    text_upward,
    text_downward,
    layout_joint,
    layout_mixing,
    layout_norms,
    layout_upward,
    layout_downward,
    text_cotangent,
    layout_cotangent,
):
    pages, slots, width_text = text_input.shape
    width_layout = layout_input.shape[2]
    text_rows = text_input.reshape(-1, width_text)
    layout_rows = layout_input.reshape(-1, width_layout)
    text_grid = (
        matmul(text_rows, text_joint).astype(jnp.bfloat16).reshape(pages, slots, 3, HEADS, -1)
    )
    layout_grid = (
        matmul(layout_rows, layout_joint).astype(jnp.bfloat16).reshape(pages, slots, 3, HEADS, -1)
    )
    text_mixed, layout_mixed, text_total, layout_total = lax.map(
        page_forward, (text_grid, layout_grid, page_counts)
    )
    text_mixed = text_mixed.reshape(-1, width_text)
    layout_mixed = layout_mixed.reshape(-1, width_layout)
    text_resid = text_rows.astype(jnp.float32) + matmul(text_mixed, text_mixing)
    layout_resid = layout_rows.astype(jnp.float32) + matmul(layout_mixed, layout_mixing)
    text_first, text_pull_one = jax.vjp(normalize, text_resid, text_norms[0], text_norms[1])
    layout_first, layout_pull_one = jax.vjp(
        normalize, layout_resid, layout_norms[0], layout_norms[1]
    )
    text_low = text_first.astype(jnp.bfloat16)
    layout_low = layout_first.astype(jnp.bfloat16)
    text_inputs, layout_inputs = (
        lax.all_gather(text_low, "tensor", axis=0, tiled=True),
        lax.all_gather(layout_low, "tensor", axis=0, tiled=True),
    )
    text_up_w, text_down_w, layout_up_w, layout_down_w = (
        text_upward,
        text_downward,
        layout_upward,
        layout_downward,
    )
    text_hidden = matmul(text_inputs, text_up_w)
    layout_hidden = matmul(layout_inputs, layout_up_w)
    text_active, text_gelu_pull = jax.vjp(gelu_exact, text_hidden)
    layout_active, layout_gelu_pull = jax.vjp(gelu_exact, layout_hidden)
    text_active = text_active.astype(jnp.bfloat16)
    layout_active = layout_active.astype(jnp.bfloat16)
    text_partial = matmul(text_active, text_down_w)
    layout_partial = matmul(layout_active, layout_down_w)
    text_feed, layout_feed = (
        lax.psum_scatter(text_partial, "tensor", scatter_dimension=0, tiled=True),
        lax.psum_scatter(layout_partial, "tensor", scatter_dimension=0, tiled=True),
    )
    text_out, text_pull_two = jax.vjp(
        normalize, text_first + text_feed, text_norms[2], text_norms[3]
    )
    layout_out, layout_pull_two = jax.vjp(
        normalize, layout_first + layout_feed, layout_norms[2], layout_norms[3]
    )
    text_result = text_out.astype(jnp.bfloat16).reshape(pages, slots, width_text)
    layout_result = layout_out.astype(jnp.bfloat16).reshape(pages, slots, width_layout)
    text_dsecond, text_dgain_two, text_dshift_two = text_pull_two(
        text_cotangent.reshape(-1, width_text).astype(jnp.float32)
    )
    layout_dsecond, layout_dgain_two, layout_dshift_two = layout_pull_two(
        layout_cotangent.reshape(-1, width_layout).astype(jnp.float32)
    )
    text_dfeed = text_dsecond.astype(jnp.bfloat16)
    layout_dfeed = layout_dsecond.astype(jnp.bfloat16)
    text_dfeed_all, layout_dfeed_all = (
        lax.all_gather(text_dfeed, "tensor", axis=0, tiled=True),
        lax.all_gather(layout_dfeed, "tensor", axis=0, tiled=True),
    )
    text_dhidden = text_gelu_pull(matmul(text_dfeed_all, text_down_w.T))[0].astype(jnp.bfloat16)
    layout_dhidden = layout_gelu_pull(matmul(layout_dfeed_all, layout_down_w.T))[0].astype(
        jnp.bfloat16
    )
    text_down_grad = matmul(text_active.T, text_dfeed_all)
    layout_down_grad = matmul(layout_active.T, layout_dfeed_all)
    text_up_grad = matmul(text_inputs.T, text_dhidden)
    layout_up_grad = matmul(layout_inputs.T, layout_dhidden)
    text_dinput = matmul(text_dhidden, text_up_w.T)
    layout_dinput = matmul(layout_dhidden, layout_up_w.T)
    text_dinput, layout_dinput = (
        lax.psum_scatter(text_dinput, "tensor", scatter_dimension=0, tiled=True),
        lax.psum_scatter(layout_dinput, "tensor", scatter_dimension=0, tiled=True),
    )
    text_up_grad, text_down_grad, layout_up_grad, layout_down_grad = (
        lax.psum(text_up_grad.astype(jnp.bfloat16), "dp").astype(jnp.float32),
        lax.psum(text_down_grad.astype(jnp.bfloat16), "dp").astype(jnp.float32),
        lax.psum(layout_up_grad.astype(jnp.bfloat16), "dp").astype(jnp.float32),
        lax.psum(layout_down_grad.astype(jnp.bfloat16), "dp").astype(jnp.float32),
    )
    text_dresid, text_dgain_one, text_dshift_one = text_pull_one(text_dsecond + text_dinput)
    layout_dresid, layout_dgain_one, layout_dshift_one = layout_pull_one(
        layout_dsecond + layout_dinput
    )
    text_datt = text_dresid.astype(jnp.bfloat16)
    layout_datt = layout_dresid.astype(jnp.bfloat16)
    text_mix_grad = matmul(text_mixed.T, text_datt)
    layout_mix_grad = matmul(layout_mixed.T, layout_datt)
    text_dmixed = (
        matmul(text_datt, text_mixing.T).astype(jnp.bfloat16).reshape(pages, slots, HEADS, -1)
    )
    layout_dmixed = (
        matmul(layout_datt, layout_mixing.T).astype(jnp.bfloat16).reshape(pages, slots, HEADS, -1)
    )
    text_djoint, layout_djoint = lax.map(
        page_backward,
        (text_grid, layout_grid, page_counts, text_total, layout_total, text_dmixed, layout_dmixed),
    )
    text_djoint = text_djoint.reshape(-1, 3 * width_text)
    layout_djoint = layout_djoint.reshape(-1, 3 * width_layout)
    text_joint_grad = matmul(text_rows.T, text_djoint)
    layout_joint_grad = matmul(layout_rows.T, layout_djoint)
    text_gradient = (text_dresid + matmul(text_djoint, text_joint.T)).reshape(
        pages, slots, width_text
    )
    layout_gradient = (layout_dresid + matmul(layout_djoint, layout_joint.T)).reshape(
        pages, slots, width_layout
    )
    text_norm_grad = jnp.stack([text_dgain_one, text_dshift_one, text_dgain_two, text_dshift_two])
    layout_norm_grad = jnp.stack(
        [layout_dgain_one, layout_dshift_one, layout_dgain_two, layout_dshift_two]
    )
    (
        text_joint_grad,
        text_mix_grad,
        text_norm_grad,
        layout_joint_grad,
        layout_mix_grad,
        layout_norm_grad,
    ) = lax.psum(
        (
            text_joint_grad,
            text_mix_grad,
            text_norm_grad,
            layout_joint_grad,
            layout_mix_grad,
            layout_norm_grad,
        ),
        ("dp", "tensor"),
    )
    return (
        text_result,
        layout_result,
        text_gradient,
        layout_gradient,
        text_joint_grad,
        text_mix_grad,
        text_norm_grad,
        text_up_grad,
        text_down_grad,
        layout_joint_grad,
        layout_mix_grad,
        layout_norm_grad,
        layout_up_grad,
        layout_down_grad,
    )


def solution(mesh):
    return jax.shard_map(
        shards,
        mesh=mesh,
        in_specs=(
            P(("dp", "tensor"), None, None),
            P(("dp", "tensor"), None, None),
            P(("dp", "tensor")),
            P(),
            P(),
            P(),
            P(None, "tensor"),
            P("tensor", None),
            P(),
            P(),
            P(),
            P(None, "tensor"),
            P("tensor", None),
            P(("dp", "tensor"), None, None),
            P(("dp", "tensor"), None, None),
        ),
        out_specs=(
            P(("dp", "tensor"), None, None),
            P(("dp", "tensor"), None, None),
            P(("dp", "tensor"), None, None),
            P(("dp", "tensor"), None, None),
            P(),
            P(),
            P(),
            P(None, "tensor"),
            P("tensor", None),
            P(),
            P(),
            P(),
            P(None, "tensor"),
            P("tensor", None),
        ),
        check_vma=False,
    )
```

profile of v0, /device:TPU:0, one launch (start us, length us, event | category | flops | bytes accessed | tf_op | source)
XLA Modules:
  0.0 606.4 jit_solution(1691573093866012901)
XLA Ops:
  7.2 1.9 copy-done
  9.2 4.5 convolution_convert_fusion
  13.7 4.3 copy.43
  18.0 7.8 %fusion.50 = f32[12,512,512]{1,2,0:T(8,128)} fusion(bf16[512,3,12,64]{0,3,2,1:T(8,128)(2,1)} %bitcast.190), kind=kOutput, calls=%fused_computation.103 | convolution fusion | flops 402653184 | bytes 14155776 | tf_op jit(solution)/shard_map/while/body/eval_jaxpr/qhd,khd->hqk/dot_general | solution.py:22
  26.9 6.8 %fusion.82 = (f32[12,512]{1,0:T(8,128)S(1)}, f32[12,512,512]{1,2,0:T(8,128)S(1)}) fusion(bf16[512,3,12,16]{0,3,2,1:T(8,128)(2,1)S(1)} %bitcast.203, f32[12,512,512]{1,2,0:T(8,128)} %fusion.50, pred[512]{0:T(512)(128)(4,1)S(1)} %iota_compare_fusion), kind=kOutput, calls=%fused_computation.171 | convolution fusion | flops 116385792 | bytes 25584128 | tf_op jit(solution)/shard_map/while/body/eval_jaxpr/qhd,khd->hqk/dot_general | solution.py:22
  33.7 1.9 exponential_reduce_fusion
  35.5 2.6 copy-done.1
  38.2 9.4 %fusion.5 = bf16[12,512,512]{1,2,0:T(8,128)(2,1)} fusion(f32[12,512,512]{1,2,0:T(8,128)} %copy-done.1, f32[12,512]{1,0:T(8,128)S(1)} %log_add_fusion), kind=kLoop, calls=%fused_computation.11 | loop fusion | flops 6291456 | bytes 18898944 | tf_op jit(solution)/shard_map/while/body/eval_jaxpr/convert_element_type | solution.py:41
  47.6 4.1 convolution_convert_fusion.4
  54.5 1.2 fusion.32
  56.0 3.9 convolution_convert_fusion.7
  61.5 2.2 all_gather.13
  63.7 4.8 multiply_convert_fusion.1
  69.4 1.3 fusion.86
  70.9 19.8 %multiply_convert_fusion = (bf16[1024,1536]{1,0:T(8,128)(2,1)S(1)}, f32[1024,1536]{1,0:T(8,128)}, f32[1024,1536]{1,0:T(8,128)}) fusion(bf16[1024,768]{1,0:T(8,128)(2,1)} %all-gather.3.cloned.1.call-done, bf16[768,1536]{1,0:T(8,128)(2,1)} %param.21), kind=kOutput, calls=%fused_computation.14 | convolution fusion | flops 2518155264 | bytes 19660800 | tf_op jit(solution)/shard_map/dot_general | solution.py:93
  90.7 1.7 copy-done.78
  92.4 4.3 fusion.85
  96.7 1.3 fusion.75
  98.8 1.7 fusion.55
  100.5 9.9 %reduce-scatter.5.cloned.1.call-done = f32[512,768]{1,0:T(8,128)} async-done(((f32[1024,768]{1,0:T(8,128)}), f32[512,768]{1,0:T(8,128)}) %reduce-scatter.5.cloned.1.call-update) | async-done | bytes 1572880 | tf_op jit(solution)/shard_map/reduce_scatter | solution.py:155
  110.4 2.5 fusion.78
  113.2 1.3 fusion.24
  114.5 1.6 fusion.74
  116.1 1.1 copy-done.7
  118.3 12.3 %reduce-scatter.11.cloned.1.call-start = ((), (), s32[]{:S(2)}) async-start(), calls=%async_computation.9 | async-start | bytes 1179648 | tf_op jit(solution)/shard_map/reduce_scatter | solution.py:190
  131.3 1.8 fusion.56
  133.2 1.2 add_convert_fusion.8
  134.4 2.1 all_gather.15
  136.5 2.9 add_convert_fusion.2
  140.4 1.3 fusion.88
  141.8 9.9 %add_convert_fusion.1 = bf16[1024,1536]{1,0:T(8,128)(2,1)S(1)} fusion(f32[1024,1536]{1,0:T(8,128)} %get-tuple-element.151, f32[1024,1536]{1,0:T(8,128)} %get-tuple-element.164, bf16[1024,768]{1,0:T(8,128)(2,1)} %all-gather.5.cloned.1.call-done, bf16[1536,768]{1,0:T(8,128)(2,1)} %param.22), kind=kOutput, calls=%fused_computation.13 | convolution fusion | flops 2437939200 | bytes 19660800 | tf_op jit(solution)/shard_map/dot_general | solution.py:93
  151.7 1.7 copy-done.76
  153.4 4.3 fusion.87
  157.8 2.3 convolution_convert_fusion.9
  160.0 2.3 convolution_convert_fusion.8
  162.3 3.0 multiply_reduce_fusion.6
  166.0 1.2 fusion.72
  168.8 5.4 convolution_bitcast_fusion.3
  174.2 7.4 %fusion.62 = f32[12,512,512]{1,2,0:T(8,128)} fusion(bf16[512,12,16]{0,2,1:T(8,128)(2,1)S(1)} %bitcast.211, bf16[512,3,12,16]{0,3,2,1:T(8,128)(2,1)} %bitcast.205), kind=kOutput, calls=%fused_computation.131 | convolution fusion | flops 100663296 | bytes 12976128 | tf_op jit(solution)/shard_map/while/body/eval_jaxpr/qhd,khd->hqk/dot_general | solution.py:59
  181.6 4.0 convolution_convert_fusion.2
  185.6 3.9 convolution_convert_fusion.1
  189.7 3.9 multiply_reduce_fusion.2
  195.4 1.7 convolution_convert_fusion.3
  197.1 2.3 copy.46
  199.5 12.8 %multiply_reduce_fusion.1 = (f32[12,512]{1,0:T(8,128)}, f32[12,512,512]{1,2,0:T(8,128)}) fusion(f32[12,512,512]{1,2,0:T(8,128)} %copy-done.1, f32[12,512]{1,0:T(8,128)} %copy-done.31, bf16[512,12,64]{0,2,1:T(8,128)(2,1)} %bitcast.197, bf16[512,3,12,64]{0,3,2,1:T(8,128)(2,1)} %bitcast.191), kind=kOutput, calls=%fused_computation.5 | convolution fusion | flops 412084224 | bytes 26796032 | tf_op jit(solution)/shard_map/while/body/eval_jaxpr/qhd,khd->hqk/dot_general | solution.py:59
  212.2 22.8 %fusion.43 = bf16[512,1,12,16]{0,3,2,1:T(8,128)(2,1)} fusion(f32[12,512,512]{1,2,0:T(8,128)} %fusion.62, f32[12,512,512]{1,2,0:T(8,128)} %get-tuple-element.169, f32[12,512,512]{1,2,0:T(8,128)} %copy-done.1, f32[12,512]{1,0:T(8,128)} %get-tuple-element.168, f32[12,512]{1,0:T(8,128)} %copy-done.31, bf16[512,3,12,16]{0,3,2,1:T(8,128)(2,1)} %bitcast.206), kind=kOutput, calls=%fused_computation.90 | convolution fusion | flops 129178112 | bytes 63406080 | tf_op jit(solution)/shard_map/while/body/eval_jaxpr/hqk,qhd->khd/dot_general | solution.py:71
  235.0 22.6 %fusion.37 = bf16[512,1,12,16]{0,3,2,1:T(8,128)(2,1)} fusion(f32[12,512,512]{1,2,0:T(8,128)} %fusion.62, f32[12,512,512]{1,2,0:T(8,128)} %get-tuple-element.169, f32[12,512,512]{1,2,0:T(8,128)} %copy-done.1, f32[12,512]{1,0:T(8,128)} %get-tuple-element.168, f32[12,512]{1,0:T(8,128)} %copy-done.31, bf16[512,3,12,16]{0,3,2,1:T(8,128)(2,1)} %bitcast.207), kind=kOutput, calls=%fused_computation.88 | convolution fusion | flops 129178112 | bytes 63406080 | tf_op jit(solution)/shard_map/while/body/eval_jaxpr/hqk,khd->qhd/dot_general | solution.py:67
  257.6 1.2 maximum_convert_fusion.1
  258.9 5.3 convolution_bitcast_fusion.1
  264.2 10.0 %fusion.2 = bf16[12,512,512]{1,2,0:T(8,128)(2,1)S(1)} fusion(f32[12,512,512]{1,2,0:T(8,128)} %get-tuple-element.169, f32[12,512,512]{1,2,0:T(8,128)} %copy-done.1, f32[12,512]{1,0:T(8,128)S(1)} %copy-done.42, f32[12,512]{1,0:T(8,128)S(1)} %copy-done.32), kind=kLoop, calls=%fused_computation.9 | loop fusion | flops 12582912 | bytes 31506432 | tf_op jit(solution)/shard_map/while/body/eval_jaxpr/convert_element_type | solution.py:84
  274.3 2.0 multiply_bitcast_fusion
  278.4 1.2 convolution_bitcast_fusion.2
  280.3 2.3 fusion.70
  282.6 5.0 convolution_bitcast_fusion
  287.6 1.3 convert_reduce_fusion
  291.8 86.3 %all-reduce.8.cloned.1.call-done = (bf16[768,1536]{1,0:T(8,128)(2,1)}, bf16[1536,768]{1,0:T(8,128)(2,1)}, bf16[192,384]{1,0:T(8,128)(2,1)}, bf16[384,192]{0,1:T(8,128)(2,1)}) async-done(((bf16[768,1536]{1,0:T(8,128)(2,1)}, bf16[1536,768]{1,0:T(8,128)(2,1)}, bf16[192,384]{1,0:T(8,128)(2,1)}, bf16[384,192]{0,1:T(8,128)(2,1)}), (bf16[768,1536]{1,0:T(8,128)(2,1)}, bf16[1536,768]{1,0:T(8,128)(2,1)}, ...) | async-done | bytes 5013520 | tf_op jit(solution)/shard_map/psum | solution.py:193
  378.2 4.6 convert_element_type.188
  382.9 2.5 convert_element_type.190
  387.0 41.7 %all-reduce = (f32[4,768]{1,0:T(4,128)}, f32[4,192]{1,0:T(4,128)}) all-reduce(f32[4,768]{1,0:T(4,128)S(1)} %pad_maximum_fusion, f32[4,192]{1,0:T(4,128)} %pad_maximum_fusion.1), channel_id=1, replica_groups=mesh['dp'=16,'tensor'=2] {'dp','tensor'}, use_global_device_ids=true, to_apply=%region_30.31 | all-reduce | flops 3840 | bytes 30720 | tf_op jit(solution)/shard_map/psum | solution.py:237
  428.7 2.3 fusion.33
  431.0 5.5 add_bitcast_fusion
  436.5 149.9 %all-reduce.6.cloned.1.call-done = (f32[768,2304]{0,1:T(8,128)}, f32[768,768]{1,0:T(8,128)}, f32[192,576]{1,0:T(8,128)}, f32[192,192]{1,0:T(8,128)}) async-done(((f32[768,2304]{0,1:T(8,128)}, f32[768,768]{1,0:T(8,128)}, f32[192,576]{1,0:T(8,128)}, f32[192,192]{1,0:T(8,128)}), (f32[768,2304]{0,1:T(8,128)}, f32[768,768]{1,0:T(8,128)}, f32[192,576]{1,0:T(8,128)}, ...) | async-done | bytes 10027024 | tf_op jit(solution)/shard_map/psum | solution.py:237
  586.4 8.0 %copy.53 = f32[768,2304]{1,0:T(8,128)} copy(f32[768,2304]{0,1:T(8,128)} %get-tuple-element.128) | data formatting | bytes 14155776
  594.3 3.3 copy.71
  (218 shorter events, 22.8 us)
Async XLA Ops:
  7.2 63.6 %all-gather.3.cloned.1.call-start = ((), (), s32[]{:S(2)}) async-start(), calls=%async_computation.4 | async-start | bytes 2359296 | tf_op jit(solution)/shard_map/all_gather | solution.py:137
  18.0 8.5 %copy-start.23 = (bf16[1,512,192]{1,2,0:T(8,128)(2,1)S(1)}, bf16[1,512,192]{1,2,0:T(8,128)(2,1)}, u32[]{:S(2)}) copy-start(bf16[1,512,192]{1,2,0:T(8,128)(2,1)} %param.16) | copy-start | bytes 589828
  18.0 8.5 %copy-start.28 = (bf16[192,576]{1,0:T(8,128)(2,1)S(1)}, bf16[192,576]{1,0:T(8,128)(2,1)}, u32[]{:S(2)}) copy-start(bf16[192,576]{1,0:T(8,128)(2,1)} %param.23) | copy-start | bytes 663556
  26.8 6.8 %copy-start.17 = (bf16[512,576]{0,1:T(8,128)(2,1)}, bf16[512,576]{0,1:T(8,128)(2,1)S(1)}, u32[]{:S(2)}) copy-start(bf16[512,576]{0,1:T(8,128)(2,1)S(1)} %convolution_convert_fusion.5) | copy-start | bytes 1769476
  33.7 4.5 copy-start.1
  38.2 9.4 %copy-start.31 = (f32[12,512]{1,0:T(8,128)}, f32[12,512]{1,0:T(8,128)S(1)}, u32[]{:S(2)}) copy-start(f32[12,512]{1,0:T(8,128)S(1)} %log_add_fusion) | copy-start | bytes 73732
  38.2 9.4 %copy-start.4 = (bf16[512,2304]{0,1:T(8,128)(2,1)S(1)}, bf16[512,2304]{0,1:T(8,128)(2,1)}, u32[]{:S(2)}) copy-start(bf16[512,2304]{0,1:T(8,128)(2,1)} %copy.43) | copy-start | bytes 7077892
  47.6 4.1 copy-start.61
  47.6 4.8 copy-start.29
  47.6 4.8 copy-start.74
  55.7 41.0 %reduce-scatter.7.cloned.1.call-start = ((), (), s32[]{:S(2)}) async-start(), calls=%async_computation.6 | async-start | bytes 1179648 | tf_op jit(solution)/shard_map/reduce_scatter | solution.py:156
  56.0 3.9 copy-start.24
  56.0 3.9 copy-start.34
  56.0 4.3 copy-start.69
  59.9 8.6 %copy-start.20 = (bf16[12,512,16]{1,2,0:T(8,128)(2,1)}, bf16[12,512,16]{1,2,0:T(8,128)(2,1)S(1)}, u32[]{:S(2)}) copy-start(bf16[12,512,16]{1,2,0:T(8,128)(2,1)S(1)} %convolution_convert_fusion.7) | copy-start | bytes 589828
  59.9 3.8 copy-start.40
  63.7 4.8 copy-start.26
  63.7 5.7 copy-start.39
  70.8 39.6 %reduce-scatter.5.cloned.1.call-start = ((), (), s32[]{:S(2)}) async-start(), calls=%async_computation.5 | async-start | bytes 4718592 | tf_op jit(solution)/shard_map/reduce_scatter | solution.py:155
  70.8 21.5 %copy-start.70 = (bf16[1536,768]{1,0:T(8,128)(2,1)S(1)}, bf16[1536,768]{1,0:T(8,128)(2,1)}, u32[]{:S(2)}) copy-start(bf16[1536,768]{1,0:T(8,128)(2,1)} %param.22) | copy-start | bytes 7077892
  96.7 45.1 %all-gather.5.cloned.1.call-start = ((), (), s32[]{:S(2)}) async-start(), calls=%async_computation.7 | async-start | bytes 2359296 | tf_op jit(solution)/shard_map/all_gather | solution.py:175
  110.3 2.8 copy-start.10
  110.3 2.8 copy-start.45
  118.3 44.1 %reduce-scatter.11.cloned.1.call-start = ((), (), s32[]{:S(2)}) async-start(), calls=%async_computation.9 | async-start | bytes 1179648 | tf_op jit(solution)/shard_map/reduce_scatter | solution.py:190
  131.3 5.1 copy-start.49
  131.3 5.1 copy-start.50
  133.2 3.3 copy-start.56
  136.5 3.0 copy-start.27
  136.5 3.9 copy-start.41
  141.7 47.9 %reduce-scatter.9.cloned.1.call-start = ((), (), s32[]{:S(2)}) async-start(), calls=%async_computation.8 | async-start | bytes 4718592 | tf_op jit(solution)/shard_map/reduce_scatter | solution.py:189
  141.8 11.6 %copy-start.71 = (bf16[768,1536]{1,0:T(8,128)(2,1)S(1)}, bf16[768,1536]{1,0:T(8,128)(2,1)}, u32[]{:S(2)}) copy-start(bf16[768,1536]{1,0:T(8,128)(2,1)} %param.21) | copy-start | bytes 7077892
  157.7 220.5 %all-reduce.8.cloned.1.call-start = ((), (), s32[]{:S(2)}) async-start(), calls=%async_computation.11 | async-start | bytes 10027008 | tf_op jit(solution)/shard_map/psum | solution.py:193
  162.3 4.9 copy-start.35
  162.3 5.6 copy-start.21
  167.2 7.0 %copy-start.47 = (f32[512]{0:T(512)}, f32[512]{0:T(512)S(1)}, u32[]{:S(2)}) copy-start(f32[512]{0:T(512)S(1)} %negate_multiply_fusion.2) | copy-start | bytes 6148
  174.2 7.4 %copy-start.72 = (bf16[1024,768]{1,0:T(8,128)(2,1)S(1)}, bf16[1024,768]{1,0:T(8,128)(2,1)}, u32[]{:S(2)}) copy-start(bf16[1024,768]{1,0:T(8,128)(2,1)} %all-gather.3.cloned.1.call-done) | copy-start | bytes 4718596
  174.2 7.4 %copy-start.77 = (bf16[1024,1536]{1,0:T(8,128)(2,1)S(1)}, bf16[1024,1536]{1,0:T(8,128)(2,1)}, u32[]{:S(2)}) copy-start(bf16[1024,1536]{1,0:T(8,128)(2,1)} %copy-done.76) | copy-start | bytes 9437188
  181.6 4.0 copy-start.73
  181.6 4.0 copy-start.79
  189.6 4.0 copy-start.53
  189.6 396.8 %all-reduce.6.cloned.1.call-start = ((), (), s32[]{:S(2)}) async-start(), calls=%async_computation.10 | async-start | bytes 20250624 | tf_op jit(solution)/shard_map/psum | solution.py:237
  189.6 3.9 copy-start.3
  194.3 85.3 %copy-start.65 = (f32[512]{0:T(512)}, f32[512]{0:T(512)S(1)}, u32[]{:S(2)}) copy-start(f32[512]{0:T(512)S(1)} %negate_multiply_fusion.4) | copy-start | bytes 6148
  258.9 18.9 %copy-start.16 = (bf16[512,3,12,16]{0,3,2,1:T(8,128)(2,1)}, bf16[512,3,12,16]{0,3,2,1:T(8,128)(2,1)S(1)}, u32[]{:S(2)}) copy-start(bf16[512,3,12,16]{0,3,2,1:T(8,128)(2,1)S(1)} %maximum_convert_fusion.1) | copy-start | bytes 1769476
  258.9 5.3 copy-start.32
  258.9 5.3 copy-start.42
  264.2 10.1 %copy-start.5 = (bf16[512,2304]{0,1:T(8,128)(2,1)S(1)}, bf16[512,2304]{0,1:T(8,128)(2,1)}, u32[]{:S(2)}) copy-start(bf16[512,2304]{0,1:T(8,128)(2,1)} %copy.43) | copy-start | bytes 7077892
  277.5 2.8 copy-start.14
  277.7 4.8 copy-start.8
  280.3 2.3 copy-start.30
  287.6 3.0 copy-start.66
  287.6 3.0 copy-start.67
  287.6 3.0 copy-start.68
  287.6 3.6 copy-start.58
  378.2 4.7 copy-start.22
  382.8 2.6 copy-start.38
  382.8 3.3 copy-start.37
  382.8 4.1 copy-start.60
  382.8 4.1 copy-start.59
  382.8 4.1 copy-start.62
  382.8 4.1 copy-start.63
  382.9 45.8 %copy-start.48 = (f32[512]{0:T(512)S(1)}, f32[512]{0:T(512)}, u32[]{:S(2)}) copy-start(f32[512]{0:T(512)} %copy-done.47) | copy-start | bytes 6148
  594.3 3.3 copy-start.33
  594.3 4.1 copy-start.36
  (24 other events, 28.6 us)
Sparse Core Ops, SparseCore 0:
  55.8 12.4 all-gather.2
  70.9 10.8 reduce-scatter.6
  96.8 13.5 reduce-scatter.4
  118.4 10.9 all-gather.4
  141.8 9.3 reduce-scatter.10
  157.8 12.0 reduce-scatter.8
  189.7 188.4 all-reduce.7
  385.7 200.6 all-reduce.5
where the time goes:
time: 616 us; the launch traced here: 606 us
  waiting for transfers between devices  246 us (40%)
  matrix products  188 us (31%)
  other arithmetic  58.9 us (10%)
  blocking collectives  45.9 us (7%)
  local copies, waits for them, and re-layouts  37.9 us (6%)
  between operations  16.1 us (3%)
  starting transfers between devices  12.9 us (2%)
    psum x1, waiting for transfers between devices, shards(): lax.psum((text_joint_grad, text_mix_grad, text_norm_grad, layout_joint_gr...  150 us
    dot_general x24, matrix products, matmul(): return jnp.dot(left, right, preferred_element_type=jnp.float32)  86.4 us
    psum x1, waiting for transfers between devices, shards(): lax.psum(text_up_grad.astype(jnp.bfloat16), 'dp').astype(jnp.float32)  86.3 us
    psum x1, blocking collectives, shards(): lax.psum((text_joint_grad, text_mix_grad, text_norm_grad, layout_joint_gr...  41.7 us
    unnamed x164, local copies, waits for them, and re-layouts  28.8 us
    dot_general x2, matrix products, joint_grads(): jnp.einsum('hqk,qhd->khd', score_grad, grid[:, 0], preferred_element_type...  24.8 us
    dot_general x2, matrix products, joint_grads(): jnp.einsum('hqk,khd->qhd', score_grad, grid[:, 1], preferred_element_type...  23.8 us
    dot_general x2, matrix products, probs_back(): jnp.einsum('qhd,khd->hqk', upstream, values, preferred_element_type=jnp.f...  20.2 us
  transfers between devices with their start and end apart: 8, of which 3 were waited for; matrix products, arithmetic and copies ran while one was open for 34% of the time, Pallas kernels for 0%

commit v1 on v0

--- a/solution.py
+++ b/solution.py
@@ -6,6 +6,10 @@
 
 HEADS = 12
 NEG_FILL = -1e30
+
+
+def produce_positions(target, group_axis, axis_tag):
+    return lax.psum(lax.psum(target, group_axis), axis_tag)
 
 
 def normalize(hidden, gain, shift):
@@ -234,7 +238,7 @@
         layout_joint_grad,
         layout_mix_grad,
         layout_norm_grad,
-    ) = lax.psum(
+    ) = produce_positions(
         (
             text_joint_grad,
             text_mix_grad,
@@ -243,7 +247,8 @@
             layout_mix_grad,
             layout_norm_grad,
         ),
-        ("dp", "tensor"),
+        "tensor",
+        "dp",
     )
     return (
         text_result,

time: 616 us -> 845 us (1.37)
  waiting for transfers between devices: 246 us -> 439 us
  blocking collectives: 45.9 us -> 87.6 us
    psum x1, waiting for transfers between devices: 86.3 us -> 193 us  [shards(): lax.psum(text_up_grad.astype(jnp.bfloat16), 'dp').astype(jnp.float32)]
    psum x1 -> x2, waiting for transfers between devices: 150 us -> 235 us  [produce_positions(): return lax.psum(lax.psum(target, group_axis), axis_tag)]
    psum x1 -> x2, blocking collectives: 41.7 us -> 83.4 us  [produce_positions(): return lax.psum(lax.psum(target, group_axis), axis_tag)]
    unnamed x164 -> x178, local copies, waits for them, and re-layouts: 28.8 us -> 29.6 us
  transfers between devices with their start and end apart: 8 -> 9, of which waited for: 3 -> 4; matrix products, arithmetic and copies ran while one was open for 34% -> 14% of each run, Pallas kernels for 0% -> 0%
where the time goes in v1:
time: 845 us; the launch traced here: 836 us
  waiting for transfers between devices  439 us (52%)
  matrix products  191 us (23%)
  blocking collectives  87.6 us (10%)
  other arithmetic  54.5 us (6%)
  local copies, waits for them, and re-layouts  38.7 us (5%)
  between operations  15.8 us (2%)
  starting transfers between devices  9.79 us (1%)
    psum x2, waiting for transfers between devices, produce_positions(): return lax.psum(lax.psum(target, group_axis), axis_tag)  235 us
    psum x1, waiting for transfers between devices, shards(): lax.psum(text_up_grad.astype(jnp.bfloat16), 'dp').astype(jnp.float32)  193 us
    dot_general x24, matrix products, matmul(): return jnp.dot(left, right, preferred_element_type=jnp.float32)  90.2 us
    psum x2, blocking collectives, produce_positions(): return lax.psum(lax.psum(target, group_axis), axis_tag)  83.4 us
    unnamed x178, local copies, waits for them, and re-layouts  29.6 us
    dot_general x2, matrix products, joint_grads(): jnp.einsum('hqk,qhd->khd', score_grad, grid[:, 0], preferred_element_type...  24.8 us
    dot_general x2, matrix products, joint_grads(): jnp.einsum('hqk,khd->qhd', score_grad, grid[:, 1], preferred_element_type...  23.9 us
    dot_general x2, matrix products, probs_back(): jnp.einsum('qhd,khd->hqk', upstream, values, preferred_element_type=jnp.f...  17.6 us
  transfers between devices with their start and end apart: 9, of which 4 were waited for; matrix products, arithmetic and copies ran while one was open for 14% of the time, Pallas kernels for 0%

profile of v1, /device:TPU:0, one launch (start us, length us, event | category | flops | bytes accessed | tf_op | source)
XLA Modules:
  0.0 836.1 jit_solution(6863856620969130872)
XLA Ops:
  7.2 1.9 copy-done
  9.2 4.5 convolution_convert_fusion
  13.7 4.3 copy.43
  18.0 7.8 fusion.50
  26.9 6.8 fusion.82
  33.7 1.9 exponential_reduce_fusion
  35.6 2.7 copy-done.1
  38.3 9.4 %fusion.5 = bf16[12,512,512]{1,2,0:T(8,128)(2,1)} fusion(f32[12,512,512]{1,2,0:T(8,128)} %copy-done.1, f32[12,512]{1,0:T(8,128)S(1)} %log_add_fusion), kind=kLoop, calls=%fused_computation.11 | loop fusion | flops 6291456 | bytes 18898944 | tf_op jit(solution)/shard_map/while/body/eval_jaxpr/convert_element_type | solution.py:45
  47.7 4.0 convolution_convert_fusion.4
  54.5 1.2 fusion.32
  56.1 3.9 convolution_convert_fusion.7
  61.5 2.1 all_gather.13
  63.7 4.8 multiply_convert_fusion.1
  69.4 1.3 fusion.86
  70.9 19.7 %multiply_convert_fusion = (bf16[1024,1536]{1,0:T(8,128)(2,1)S(1)}, f32[1024,1536]{1,0:T(8,128)}, f32[1024,1536]{1,0:T(8,128)}) fusion(bf16[1024,768]{1,0:T(8,128)(2,1)} %all-gather.3.cloned.1.call-done, bf16[768,1536]{1,0:T(8,128)(2,1)} %param.21), kind=kOutput, calls=%fused_computation.14 | convolution fusion | flops 2518155264 | bytes 19660800 | tf_op jit(solution)/shard_map/dot_general | solution.py:97
  90.5 1.6 copy-done.82
  92.1 4.3 fusion.85
  96.5 1.3 fusion.75
  98.6 1.6 fusion.55
  100.2 9.9 %reduce-scatter.5.cloned.1.call-done = f32[512,768]{1,0:T(8,128)} async-done(((f32[1024,768]{1,0:T(8,128)}), f32[512,768]{1,0:T(8,128)}) %reduce-scatter.5.cloned.1.call-update) | async-done | bytes 1572880 | tf_op jit(solution)/shard_map/reduce_scatter | solution.py:159
  110.1 2.5 fusion.78
  113.0 1.3 fusion.24
  114.3 1.6 fusion.74
  118.1 9.2 %reduce-scatter.11.cloned.1.call-start = ((), (), s32[]{:S(2)}) async-start(), calls=%async_computation.9 | async-start | bytes 1179648 | tf_op jit(solution)/shard_map/reduce_scatter | solution.py:194
  128.0 1.8 fusion.56
  129.8 1.2 add_convert_fusion.8
  131.0 2.1 all_gather.15
  133.1 2.9 add_convert_fusion.2
  137.0 1.3 fusion.88
  138.4 9.9 %add_convert_fusion.1 = bf16[1024,1536]{1,0:T(8,128)(2,1)S(1)} fusion(f32[1024,1536]{1,0:T(8,128)} %get-tuple-element.157, f32[1024,1536]{1,0:T(8,128)} %get-tuple-element.170, bf16[1024,768]{1,0:T(8,128)(2,1)} %all-gather.5.cloned.1.call-done, bf16[1536,768]{1,0:T(8,128)(2,1)} %param.22), kind=kOutput, calls=%fused_computation.13 | convolution fusion | flops 2437939200 | bytes 19660800 | tf_op jit(solution)/shard_map/dot_general | solution.py:97
  148.4 1.7 copy-done.81
  150.0 4.3 fusion.87
  154.5 3.0 multiply_reduce_fusion.6
  158.1 1.2 fusion.72
  161.0 6.0 convolution_bitcast_fusion.3
  167.0 7.2 fusion.62
  174.2 3.9 multiply_reduce_fusion.2
  180.0 1.7 convolution_convert_fusion.3
  181.7 2.3 copy.46
  184.0 6.1 convolution_bitcast_fusion.1
  190.1 10.4 %multiply_reduce_fusion.1 = (f32[12,512]{1,0:T(8,128)S(1)}, f32[12,512,512]{1,2,0:T(8,128)}) fusion(f32[12,512,512]{1,2,0:T(8,128)} %copy-done.1, f32[12,512]{1,0:T(8,128)S(1)} %copy-done.35, bf16[512,12,64]{0,2,1:T(8,128)(2,1)S(1)} %bitcast.200, bf16[512,3,12,64]{0,3,2,1:T(8,128)(2,1)S(1)} %bitcast.194), kind=kOutput, calls=%fused_computation.5 | convolution fusion | flops 412084224 | bytes 26796032 | tf_op jit(solution)/shard_map/while/body/eval_jaxpr/qhd,khd->hqk/dot_general | solution.py:63
  201.0 6.8 fusion.2
  207.9 2.9 multiply_bitcast_fusion
  210.8 2.0 multiply_bitcast_fusion.1
  212.8 21.9 %fusion.43 = bf16[512,1,12,16]{0,3,2,1:T(8,128)(2,1)} fusion(f32[12,512,512]{1,2,0:T(8,128)} %fusion.62, f32[12,512,512]{1,2,0:T(8,128)} %get-tuple-element.175, f32[12,512,512]{1,2,0:T(8,128)} %copy-done.1, f32[12,512]{1,0:T(8,128)} %copy-done.47, f32[12,512]{1,0:T(8,128)} %copy-done.34, bf16[512,3,12,16]{0,3,2,1:T(8,128)(2,1)} %bitcast.208), kind=kOutput, calls=%fused_computation.90 | convolution fusion | flops 129178112 | bytes 63406080 | tf_op jit(solution)/shard_map/while/body/eval_jaxpr/hqk,qhd->khd/dot_general | solution.py:75
  234.7 21.9 %fusion.37 = bf16[512,1,12,16]{0,3,2,1:T(8,128)(2,1)} fusion(f32[12,512,512]{1,2,0:T(8,128)} %fusion.62, f32[12,512,512]{1,2,0:T(8,128)} %get-tuple-element.175, f32[12,512,512]{1,2,0:T(8,128)} %copy-done.1, f32[12,512]{1,0:T(8,128)} %copy-done.47, f32[12,512]{1,0:T(8,128)} %copy-done.34, bf16[512,3,12,16]{0,3,2,1:T(8,128)(2,1)} %bitcast.209), kind=kOutput, calls=%fused_computation.88 | convolution fusion | flops 129178112 | bytes 63406080 | tf_op jit(solution)/shard_map/while/body/eval_jaxpr/hqk,khd->qhd/dot_general | solution.py:71
  256.7 4.1 fusion.70
  261.9 5.0 convolution_bitcast_fusion
  269.1 2.4 convolution_convert_fusion.9
  271.5 2.3 convolution_convert_fusion.8
  273.8 6.2 convolution_convert_fusion.2
  280.0 3.9 convolution_convert_fusion.1
  284.0 28.8 %all-reduce.11.cloned.1.call-done = (f32[768,2304]{0,1:T(8,128)}, f32[768,768]{1,0:T(8,128)}, f32[192,576]{1,0:T(8,128)}, f32[192,192]{1,0:T(8,128)}) async-done(((f32[768,2304]{0,1:T(8,128)}, f32[768,768]{1,0:T(8,128)}, f32[192,576]{1,0:T(8,128)}, f32[192,192]{1,0:T(8,128)}), (f32[768,2304]{0,1:T(8,128)}, f32[768,768]{1,0:T(8,128)}, f32[192,576]{1,0:T(8,128)}, ...) | async-done | bytes 10027024 | tf_op jit(solution)/shard_map/psum | solution.py:12
  312.8 1.3 convert_reduce_fusion
  317.0 192.9 %all-reduce.13.cloned.1.call-done = (bf16[768,1536]{1,0:T(8,128)(2,1)}, bf16[1536,768]{1,0:T(8,128)(2,1)}, bf16[192,384]{1,0:T(8,128)(2,1)}, bf16[384,192]{0,1:T(8,128)(2,1)}) async-done(((bf16[768,1536]{1,0:T(8,128)(2,1)}, bf16[1536,768]{1,0:T(8,128)(2,1)}, bf16[192,384]{1,0:T(8,128)(2,1)}, bf16[384,192]{0,1:T(8,128)(2,1)}), (bf16[768,1536]{1,0:T(8,128)(2,1)}, bf16[1536,768]{1,0:T(8,128)(2,1)}, ...) | async-done | bytes 5013520 | tf_op jit(solution)/shard_map/psum | solution.py:197
  509.9 4.6 convert_element_type.188
  514.6 2.5 convert_element_type.190
  518.7 4.6 all-reduce.2
  523.3 78.8 %all-reduce = (f32[4,768]{1,0:T(4,128)}, f32[4,192]{1,0:T(4,128)}) all-reduce(f32[4,768]{1,0:T(4,128)} %get-tuple-element.132, f32[4,192]{1,0:T(4,128)} %get-tuple-element.133), channel_id=1, replica_groups=mesh['dp'=16,'tensor'=2] {'dp'}, use_global_device_ids=true, to_apply=%region_33.34 | all-reduce | flops 3840 | bytes 30720 | tf_op jit(solution)/shard_map/psum | solution.py:12
  602.1 2.3 fusion.33
  604.4 5.4 add_bitcast_fusion
  609.7 206.6 %all-reduce.9.cloned.1.call-done = (f32[768,2304]{0,1:T(8,128)}, f32[768,768]{1,0:T(8,128)}, f32[192,576]{1,0:T(8,128)}, f32[192,192]{1,0:T(8,128)}) async-done(((f32[768,2304]{0,1:T(8,128)}, f32[768,768]{1,0:T(8,128)}, f32[192,576]{1,0:T(8,128)}, f32[192,192]{1,0:T(8,128)}), (f32[768,2304]{0,1:T(8,128)}, f32[768,768]{1,0:T(8,128)}, f32[192,576]{1,0:T(8,128)}, ...) | async-done | bytes 10027024 | tf_op jit(solution)/shard_map/psum | solution.py:12
  816.4 8.0 copy.53
  824.3 3.3 copy.75
  (237 shorter events, 25.0 us)
Async XLA Ops:
  7.2 63.6 %all-gather.3.cloned.1.call-start = ((), (), s32[]{:S(2)}) async-start(), calls=%async_computation.4 | async-start | bytes 2359296 | tf_op jit(solution)/shard_map/all_gather | solution.py:141
  18.0 8.5 %copy-start.25 = (bf16[1,512,192]{1,2,0:T(8,128)(2,1)S(1)}, bf16[1,512,192]{1,2,0:T(8,128)(2,1)}, u32[]{:S(2)}) copy-start(bf16[1,512,192]{1,2,0:T(8,128)(2,1)} %param.16) | copy-start | bytes 589828
  18.0 8.5 %copy-start.30 = (bf16[192,576]{1,0:T(8,128)(2,1)S(1)}, bf16[192,576]{1,0:T(8,128)(2,1)}, u32[]{:S(2)}) copy-start(bf16[192,576]{1,0:T(8,128)(2,1)} %param.23) | copy-start | bytes 663556
  26.9 6.8 copy-start.16
  33.7 4.5 copy-start.1
  38.2 9.4 %copy-start.34 = (f32[12,512]{1,0:T(8,128)}, f32[12,512]{1,0:T(8,128)S(1)}, u32[]{:S(2)}) copy-start(f32[12,512]{1,0:T(8,128)S(1)} %log_add_fusion) | copy-start | bytes 73732
  38.3 9.4 %copy-start.4 = (bf16[512,2304]{0,1:T(8,128)(2,1)S(1)}, bf16[512,2304]{0,1:T(8,128)(2,1)}, u32[]{:S(2)}) copy-start(bf16[512,2304]{0,1:T(8,128)(2,1)} %copy.43) | copy-start | bytes 7077892
  47.7 4.1 copy-start.66
  47.7 4.8 copy-start.32
  47.7 4.8 copy-start.79
  55.7 40.8 %reduce-scatter.7.cloned.1.call-start = ((), (), s32[]{:S(2)}) async-start(), calls=%async_computation.6 | async-start | bytes 1179648 | tf_op jit(solution)/shard_map/reduce_scatter | solution.py:160
  56.0 3.9 copy-start.26
  56.0 3.9 copy-start.37
  56.1 4.3 copy-start.74
  59.9 8.5 %copy-start.22 = (bf16[12,512,16]{1,2,0:T(8,128)(2,1)}, bf16[12,512,16]{1,2,0:T(8,128)(2,1)S(1)}, u32[]{:S(2)}) copy-start(bf16[12,512,16]{1,2,0:T(8,128)(2,1)S(1)} %convolution_convert_fusion.7) | copy-start | bytes 589828
  60.0 3.7 copy-start.45
  63.7 4.8 copy-start.28
  63.7 5.7 copy-start.44
  70.8 39.4 %reduce-scatter.5.cloned.1.call-start = ((), (), s32[]{:S(2)}) async-start(), calls=%async_computation.5 | async-start | bytes 4718592 | tf_op jit(solution)/shard_map/reduce_scatter | solution.py:159
  70.8 21.3 %copy-start.75 = (bf16[1536,768]{1,0:T(8,128)(2,1)S(1)}, bf16[1536,768]{1,0:T(8,128)(2,1)}, u32[]{:S(2)}) copy-start(bf16[1536,768]{1,0:T(8,128)(2,1)} %param.22) | copy-start | bytes 7077892
  96.4 42.0 %all-gather.5.cloned.1.call-start = ((), (), s32[]{:S(2)}) async-start(), calls=%async_computation.7 | async-start | bytes 2359296 | tf_op jit(solution)/shard_map/all_gather | solution.py:179
  118.1 36.4 %reduce-scatter.11.cloned.1.call-start = ((), (), s32[]{:S(2)}) async-start(), calls=%async_computation.9 | async-start | bytes 1179648 | tf_op jit(solution)/shard_map/reduce_scatter | solution.py:194
  128.0 5.1 copy-start.54
  128.0 5.1 copy-start.55
  129.8 3.3 copy-start.61
  133.1 3.9 copy-start.46
  138.3 35.9 %reduce-scatter.9.cloned.1.call-start = ((), (), s32[]{:S(2)}) async-start(), calls=%async_computation.8 | async-start | bytes 4718592 | tf_op jit(solution)/shard_map/reduce_scatter | solution.py:193
  138.4 11.6 %copy-start.76 = (bf16[768,1536]{1,0:T(8,128)(2,1)S(1)}, bf16[768,1536]{1,0:T(8,128)(2,1)}, u32[]{:S(2)}) copy-start(bf16[768,1536]{1,0:T(8,128)(2,1)} %param.21) | copy-start | bytes 7077892
  154.4 158.4 %all-reduce.11.cloned.1.call-start = ((), (), s32[]{:S(2)}) async-start(), calls=%async_computation.11 | async-start | bytes 20250624 | tf_op jit(solution)/shard_map/psum | solution.py:12
  154.4 4.9 copy-start.38
  154.4 5.6 copy-start.23
  159.3 7.7 copy-start.52
  174.2 3.9 copy-start.58
  174.2 3.9 copy-start.3
  178.8 77.8 %copy-start.70 = (f32[512]{0:T(512)}, f32[512]{0:T(512)S(1)}, u32[]{:S(2)}) copy-start(f32[512]{0:T(512)S(1)} %negate_multiply_fusion.4) | copy-start | bytes 6148
  184.0 6.1 copy-start.5
  184.0 6.1 copy-start.10
  184.0 6.1 copy-start.35
  184.0 16.5 %slice-start = ((s8[12582912]{0:T(1024)(128)(4,1)}), s8[4194304]{0:T(1024)(128)(4,1)S(1)}, s32[]{:S(2)}) async-start(s8[12582912]{0:T(1024)(128)(4,1)} %bitcast.190), calls=%async_computation.13 | async-start | bytes 8388608
  190.0 10.4 %slice-start.1 = ((s8[12582912]{0:T(1024)(128)(4,1)}), s8[4194304]{0:T(1024)(128)(4,1)S(1)}, s32[]{:S(2)}) async-start(s8[12582912]{0:T(1024)(128)(4,1)} %bitcast.190), calls=%async_computation.14 | async-start | bytes 8388608
  190.1 11.0 %slice-start.2 = ((s8[12582912]{0:T(1024)(128)(4,1)}), s8[4194304]{0:T(1024)(128)(4,1)S(1)}, s32[]{:S(2)}) async-start(s8[12582912]{0:T(1024)(128)(4,1)} %bitcast.190), calls=%async_computation.15 | async-start | bytes 8388608
  200.4 7.4 copy-start.47
  256.6 4.1 copy-start.19
  256.7 4.1 copy-start.20
  256.7 4.1 copy-start.21
  261.1 5.9 copy-start.8
  261.9 5.1 copy-start.31
  261.9 5.1 copy-start.39
  261.9 5.1 copy-start.40
  261.9 5.9 copy-start.27
  269.0 240.8 %all-reduce.13.cloned.1.call-start = ((), (), s32[]{:S(2)}) async-start(), calls=%async_computation.12 | async-start | bytes 10027008 | tf_op jit(solution)/shard_map/psum | solution.py:197
  269.1 4.7 copy-start.77
  273.8 6.2 copy-start.78
  273.8 6.2 copy-start.83
  284.0 532.4 %all-reduce.9.cloned.1.call-start = ((), (), s32[]{:S(2)}) async-start(), calls=%async_computation.10 | async-start | bytes 20250624 | tf_op jit(solution)/shard_map/psum | solution.py:12
  312.8 3.6 copy-start.63
  509.9 4.7 copy-start.24
  514.5 3.3 copy-start.42
  514.5 4.1 copy-start.65
  514.5 4.1 copy-start.64
  514.6 4.1 copy-start.67
  514.6 4.1 copy-start.68
  514.6 87.5 %copy-start.53 = (f32[512]{0:T(512)S(1)}, f32[512]{0:T(512)}, u32[]{:S(2)}) copy-start(f32[512]{0:T(512)} %copy-done.52) | copy-start | bytes 6148
  824.3 4.1 copy-start.41
  (32 other events, 50.7 us)
Sparse Core Ops, SparseCore 0:
  55.8 12.4 all-gather.2
  70.9 10.8 reduce-scatter.6
  96.6 13.5 reduce-scatter.4
  118.2 10.9 all-gather.4
  138.5 9.4 reduce-scatter.10
  154.5 12.0 reduce-scatter.8
  269.2 43.5 all-reduce.10
  321.4 188.4 all-reduce.12
  517.5 298.8 all-reduce.8
